TPU v7x, 32 devices: a whole 2x2x4 slice. The times are simulated.
32 devices in a mesh: seq: 8 (over z, y), dp: 4 (over x, core).
Axes of the slice: x: 2, y: 2, z: 4, core: 2. Of those that a mesh axis runs over, the one named last changes fastest.
Arguments:
- block_input: bfloat16 [4, 1024, 1536], P('dp', 'seq'), may hold values from -6 to 6
- query_proj: bfloat16 [4, 1024, 768], P('dp', 'seq'), may hold values from -8 to 8
- key_proj: bfloat16 [4, 1024, 768], P('dp', 'seq'), may hold values from -8 to 8
- value_proj: bfloat16 [4, 1024, 768], P('dp', 'seq'), may hold values from -6 to 6
- lengths: int32 [4], P('dp'), may hold values from 256 to 1024, as said below
- out_proj: bfloat16 [1536, 768], replicated, may hold values from -0.21875 to 0.21875
- kernel: float32 [31, 1536], replicated, may hold values from -1 to 1
- conv_bias: float32 [1536], replicated, may hold values from -3 to 3
- grad_output: bfloat16 [4, 1024, 1536], P('dp', 'seq'), may hold values from -6 to 6
Outputs:
- block_output: bfloat16 [4, 1024, 1536], P('dp', 'seq')
- grad_input: bfloat16 [4, 1024, 1536], P('dp', 'seq')
- grad_query: bfloat16 [4, 1024, 768], P('dp', 'seq')
- grad_out_proj: float32 [1536, 768], P('seq')
- grad_kernel: float32 [31, 1536], P(None, 'seq')
- grad_bias: float32 [1536], P('seq')
Inputs may be any that keep to these rules, and one draw needn't show every extreme that they name: `lengths`: frames at or after an utterance's length are padding; in every draw at least one utterance has all 1024 frames valid.
All inputs are finite; a program needn't handle non-finite values.
Results may differ from a plain program's by a relative error of at most 0.012.
The roundings to bfloat16 on the way count: a program that leaves them out, or rounds other values in their place, can miss the bound.
Values may be sent and summed in bfloat16 or wider, within the bound.
No kernel may reach another device: no remote copies, remote signals or barrier semaphores. Data moves between devices by JAX's collectives and lax.ppermute only.
A program may use at most 128 MiB of HBM per device.

v0:
```python
import math
import jax
import jax.numpy as jnp
from jax import lax
from jax.sharding import PartitionSpec as P

D = 1536
H = 8
HS = 96
KW = 31
HD = 768


def with_halo(x, sides, width):
    for axis, dim in sides:
        size, length = (lax.axis_size(axis), x.shape[dim])
        up = [(i, (i + 1) % size) for i in range(size - 1)]
        down = [(j, i) for i, j in up]
        last = lax.slice_in_dim(x, length - width, length, axis=dim)
        leading = lax.slice_in_dim(x, 0, width, axis=dim)
        before = lax.ppermute(last, axis, up)
        after = lax.ppermute(leading, axis, down)
        x = jnp.concatenate([before, x, after], axis=dim)
    return x


def forward_rows(query_one, key_one, value_one, key_valid, score_scale):
    row_total = query_one.shape[0]
    block_rows = math.gcd(row_total, 512)
    query_blocks = query_one.reshape(row_total // block_rows, block_rows, query_one.shape[1])

    def forward_one_block(query_block):
        scores = (
            lax.dot_general(
                query_block, key_one, (((1,), (1,)), ((), ())), preferred_element_type=jnp.float32
            )
            * score_scale
        )
        scores = jnp.where(key_valid[None, :], scores, -jnp.inf)
        row_top = jnp.max(scores, axis=-1, keepdims=True)
        log_total = row_top + jnp.log(jnp.sum(jnp.exp(scores - row_top), axis=-1, keepdims=True))
        weights = jnp.exp(scores - log_total).astype(jnp.bfloat16)
        return (jnp.dot(weights, value_one, preferred_element_type=jnp.float32), log_total[:, 0])

    outputs, log_totals = lax.map(forward_one_block, query_blocks)
    return (outputs.reshape(row_total, query_one.shape[1]), log_totals.reshape(row_total))


def backward_rows(
    query_one, key_one, value_one, grad_one, lse_one, delta_one, key_valid, score_scale
):
    row_total = query_one.shape[0]
    block_rows = math.gcd(row_total, 512)
    block_count = row_total // block_rows
    width = query_one.shape[1]

    def backward_one_block(items):
        query_block, grad_block, lse_block, delta_block = items
        scores = (
            lax.dot_general(
                query_block, key_one, (((1,), (1,)), ((), ())), preferred_element_type=jnp.float32
            )
            * score_scale
        )
        scores = jnp.where(key_valid[None, :], scores, -jnp.inf)
        probs = jnp.exp(scores - lse_block[:, None])
        grad_prob = lax.dot_general(
            grad_block, value_one, (((1,), (1,)), ((), ())), preferred_element_type=jnp.float32
        )
        grad_score = (probs * (grad_prob - delta_block[:, None])).astype(jnp.bfloat16)
        return jnp.dot(grad_score, key_one, preferred_element_type=jnp.float32) * score_scale

    results = lax.map(
        backward_one_block,
        (
            query_one.reshape(block_count, block_rows, width),
            grad_one.reshape(block_count, block_rows, width),
            lse_one.reshape(block_count, block_rows),
            delta_one.reshape(block_count, block_rows),
        ),
    )
    return results.reshape(row_total, width)


def on_device(
    block_input, query_proj, key_proj, value_proj, lengths, out_proj, kernel, conv_bias, grad_output
):
    frames_dev = block_input.shape[1]
    seq_count = lax.axis_size("seq")
    total_frames = frames_dev * seq_count
    first_frame = lax.axis_index("seq") * frames_dev
    utt_length = lengths[0]
    local_valid = first_frame + jnp.arange(frames_dev) < utt_length
    all_valid = jnp.arange(total_frames) < utt_length
    score_scale = 1.0 / math.sqrt(HS)
    halo_width = KW // 2
    group_size = seq_count // H
    sub_rows = frames_dev // group_size
    query_local = query_proj[0]

    def to_serving(matrix):
        return matrix.reshape(frames_dev, H, HS).transpose(1, 0, 2).reshape(seq_count, sub_rows, HS)

    def from_serving(returned):
        return returned.reshape(H, frames_dev, HS).transpose(1, 0, 2).reshape(frames_dev, HD)

    query_mine = lax.all_to_all(
        to_serving(query_local), "seq", split_axis=0, concat_axis=1, tiled=True
    )[0]
    key_send = jnp.repeat(
        key_proj[0].reshape(frames_dev, H, HS).transpose(1, 0, 2), group_size, axis=0
    )
    value_send = jnp.repeat(
        value_proj[0].reshape(frames_dev, H, HS).transpose(1, 0, 2), group_size, axis=0
    )
    key_mine, value_mine = (
        lax.all_to_all(key_send, "seq", split_axis=0, concat_axis=1, tiled=True),
        lax.all_to_all(value_send, "seq", split_axis=0, concat_axis=1, tiled=True),
    )
    key_mine = key_mine[0]
    value_mine = value_mine[0]
    head_out, head_lse = forward_rows(query_mine, key_mine, value_mine, all_valid, score_scale)
    head_attended = head_out.astype(jnp.bfloat16)
    attended = from_serving(
        lax.all_to_all(head_attended[None], "seq", split_axis=1, concat_axis=0, tiled=True)
    )
    projected = lax.dot_general(
        attended, out_proj, (((1,), (1,)), ((), ())), preferred_element_type=jnp.float32
    )
    mixed_rows = (block_input[0].astype(jnp.float32) + projected).astype(jnp.bfloat16)
    masked = jnp.where(local_valid[:, None], mixed_rows, jnp.zeros_like(mixed_rows))
    padded = with_halo(masked, (("seq", 0),), halo_width).astype(jnp.float32)
    conv_rows = jnp.broadcast_to(conv_bias, (frames_dev, D))
    for tap in range(KW):
        conv_rows = conv_rows + kernel[tap] * padded[tap : tap + frames_dev]
    gate_rows = jax.nn.sigmoid(conv_rows)
    block_output = jnp.where(
        local_valid[:, None], mixed_rows.astype(jnp.float32) + conv_rows * gate_rows, 0.0
    ).astype(jnp.bfloat16)
    grad_rows = jnp.where(local_valid[:, None], grad_output[0].astype(jnp.float32), 0.0)
    grad_conv = grad_rows * gate_rows * (1.0 + conv_rows * (1.0 - gate_rows))
    kernel_local = jnp.stack(
        [jnp.sum(grad_conv * padded[tap : tap + frames_dev], axis=0) for tap in range(KW)]
    )
    bias_local = jnp.sum(grad_conv, axis=0)
    grad_padded = with_halo(grad_conv, (("seq", 0),), halo_width)
    grad_masked = jnp.zeros((frames_dev, D), jnp.float32)
    for tap in range(KW):
        begin = 2 * halo_width - tap
        grad_masked = grad_masked + kernel[tap] * grad_padded[begin : begin + frames_dev]
    grad_input = (grad_rows + jnp.where(local_valid[:, None], grad_masked, 0.0)).astype(
        jnp.bfloat16
    )
    grad_attn = jnp.dot(grad_input, out_proj, preferred_element_type=jnp.float32).astype(
        jnp.bfloat16
    )
    grad_mine = lax.all_to_all(
        to_serving(grad_attn), "seq", split_axis=0, concat_axis=1, tiled=True
    )[0]
    delta_mine = jnp.sum(grad_mine.astype(jnp.float32) * head_attended.astype(jnp.float32), axis=-1)
    grad_q_mine = backward_rows(
        query_mine, key_mine, value_mine, grad_mine, head_lse, delta_mine, all_valid, score_scale
    ).astype(jnp.bfloat16)
    grad_query = from_serving(
        lax.all_to_all(grad_q_mine[None], "seq", split_axis=1, concat_axis=0, tiled=True)
    )
    term_block = lax.dot_general(
        grad_input, attended, (((0,), (0,)), ((), ())), preferred_element_type=jnp.float32
    )
    partial_rows = lax.psum_scatter(term_block, "seq", scatter_dimension=0, tiled=True)
    summed = lax.psum(partial_rows.astype(jnp.bfloat16), "dp").astype(jnp.float32)
    kernel_total, bias_total = lax.psum((kernel_local, bias_local), ("seq", "dp"))
    shard_width = D // seq_count
    offset = lax.axis_index("seq") * shard_width
    grad_kernel = lax.dynamic_slice_in_dim(kernel_total, offset, shard_width, 1)
    grad_bias = lax.dynamic_slice_in_dim(bias_total, offset, shard_width, 0)
    return (block_output[None], grad_input[None], grad_query[None], summed, grad_kernel, grad_bias)


def solution(mesh):
    placed = (
        P("dp", "seq", None),
        P("dp", "seq", None),
        P("dp", "seq", None),
        P("dp", "seq", None),
        P("dp"),
        P(),
        P(),
        P(),
        P("dp", "seq", None),
    )
    return jax.shard_map(
        on_device,
        mesh=mesh,
        in_specs=placed,
        out_specs=(
            P("dp", "seq", None),
            P("dp", "seq", None),
            P("dp", "seq", None),
            P("seq", None),
            P(None, "seq"),
            P("seq"),
        ),
        check_vma=False,
    )
```

profile of v0, /device:TPU:0, one launch (start us, length us, event | category | flops | bytes accessed | tf_op | source)
XLA Modules:
  0.0 321.5 jit_solution(12944451114000263372)
XLA Ops:
  9.9 7.3 %all-to-all-start = ((bf16[8,128,96]{1,2,0:T(8,128)(2,1)}), bf16[8,128,96]{1,2,0:T(8,128)(2,1)S(1)}, u32[]{:S(2)}, u32[]{:S(2)}) async-start(bf16[8,128,96]{1,2,0:T(8,128)(2,1)} %bitcast.3), calls=%async_computation | async-start | bytes 393216 | tf_op jit(solution)/shard_map/all_to_all | solution.py:107
  18.9 6.2 %all-to-all-done = bf16[8,128,96]{1,2,0:T(8,128)(2,1)S(1)} async-done(((bf16[8,128,96]{1,2,0:T(8,128)(2,1)}), bf16[8,128,96]{1,2,0:T(8,128)(2,1)S(1)}, u32[]{:S(2)}, u32[]{:S(2)}) %all-to-all-start) | async-done | bytes 196640 | tf_op jit(solution)/shard_map/all_to_all | solution.py:107
  25.1 3.4 %all-to-all-start.1 = ((bf16[8,128,96]{1,2,0:T(8,128)(2,1)}), bf16[8,128,96]{1,2,0:T(8,128)(2,1)S(1)}, u32[]{:S(2)}, u32[]{:S(2)}) async-start(bf16[8,128,96]{1,2,0:T(8,128)(2,1)} %bitcast.5), calls=%async_computation.1 | async-start | bytes 393216 | tf_op jit(solution)/shard_map/all_to_all | solution.py:117
  30.3 6.0 %all-to-all-done.1 = bf16[8,128,96]{1,2,0:T(8,128)(2,1)S(1)} async-done(((bf16[8,128,96]{1,2,0:T(8,128)(2,1)}), bf16[8,128,96]{1,2,0:T(8,128)(2,1)S(1)}, u32[]{:S(2)}, u32[]{:S(2)}) %all-to-all-start.1) | async-done | bytes 196640 | tf_op jit(solution)/shard_map/all_to_all | solution.py:117
  36.3 3.4 %all-to-all-start.2 = ((bf16[8,128,96]{1,2,0:T(8,128)(2,1)}), bf16[8,128,96]{1,2,0:T(8,128)(2,1)S(1)}, u32[]{:S(2)}, u32[]{:S(2)}) async-start(bf16[8,128,96]{1,2,0:T(8,128)(2,1)} %bitcast.7), calls=%async_computation.2 | async-start | bytes 393216 | tf_op jit(solution)/shard_map/all_to_all | solution.py:118
  40.0 7.3 %all-to-all-done.2 = bf16[8,128,96]{1,2,0:T(8,128)(2,1)S(1)} async-done(((bf16[8,128,96]{1,2,0:T(8,128)(2,1)}), bf16[8,128,96]{1,2,0:T(8,128)(2,1)S(1)}, u32[]{:S(2)}, u32[]{:S(2)}) %all-to-all-start.2) | async-done | bytes 196640 | tf_op jit(solution)/shard_map/all_to_all | solution.py:118
  47.6 4.6 %while.24 = (s32[]{:T(128)}, bf16[2,512,96]{1,2,0:T(8,128)(2,1)S(1)}, f32[2,512]{1,0:T(2,128)S(1)}, bf16[2,512,96]{2,1,0:T(8,128)(2,1)S(1)}, bf16[1024,96]{1,0:T...) while((s32[]{:T(128)}, ...), condition=%wide.region_3.4_spmd.clone, body=%wide.region_0.3_spmd.clone.sunk | while | flops 204997120 | bytes 7164021 | solution.py:45
  53.2 2.6 reshape.122
  56.3 3.7 %reduce.63 = bf16[1024,96]{1,0:T(8,128)(2,1)} reduce(bf16[1024,1,96]{2,1,0:T(2,128)(2,1)} %bitcast.115, bf16[]{:T(256)} %broadcast.73), dimensions={1}, to_apply=%bitcast.66.reduce_sub_computation | reduce | bytes 393218
  62.1 3.4 %all-to-all-start.3 = ((bf16[8,2,6144]{2,1,0:T(2,128)(2,1)}), bf16[8,2,6144]{2,1,0:T(2,128)(2,1)S(1)}, u32[]{:S(2)}, u32[]{:S(2)}) async-start(bf16[8,2,6144]{2,1,0:T(2,128)(2,1)} %reshape.155), calls=%async_computation.3 | async-start | bytes 393216 | tf_op jit(solution)/shard_map/all_to_all | solution.py:125
  66.8 2.5 slice_reduce_fusion.30
  69.3 3.9 %all-to-all-done.3 = bf16[8,2,6144]{2,1,0:T(2,128)(2,1)S(1)} async-done(((bf16[8,2,6144]{2,1,0:T(2,128)(2,1)}), bf16[8,2,6144]{2,1,0:T(2,128)(2,1)S(1)}, u32[]{:S(2)}, u32[]{:S(2)}) %all-to-all-start.3) | async-done | bytes 196640 | tf_op jit(solution)/shard_map/all_to_all | solution.py:125
  75.9 2.7 broadcast_select_fusion
  83.5 3.0 collective-permute-done.1
  86.9 7.5 %multiply_reduce_fusion = (f32[1536]{0:T(1024)}, f32[1536]{0:T(1024)}, f32[1536]{0:T(1024)}, f32[1536]{0:T(1024)}, f32[1536]{0:T(1024)}, /*index=5*/f32[1536]{0:...) fusion(f32[158,1536]{1,0:T(8,128)S(1)} %maximum_convert_fusion,, ...), kind=kLoop, calls=%fused_computation.190 | loop fusion | flops 21206016 | bytes 26652800 | tf_op jit(solution)/shard_map/reduce_sum | solution.py:143
  95.7 5.0 %collective-permute-start.3 = (f32[15,1536]{1,0:T(8,128)S(1)}, f32[15,1536]{1,0:T(8,128)S(1)}, u32[]{:S(2)}, u32[]{:S(2)}) collective-permute-start(f32[15,1536]{1,0:T(8,128)S(1)} %get-tuple-element.306), channel_id=1, source_target_pairs={{0,4},{4,8},{8,12},{12,16},{16,20},{20,24},{24,28},{1,5},{5,9},{9,... | collective-permute-start | bytes 276488 | tf_op jit(solution)/shard_map/ppermute | solution.py:21
  102.7 3.7 %fusion.37 = bf16[128,1536]{1,0:T(8,128)(2,1)S(1)} fusion(f32[128,1536]{1,0:T(8,128)S(1)} %get-tuple-element.299, f32[15,1536]{1,0:T(8,128)S(1)} %collective-permute-done.3, f32[15,1536]{1,0:T(8,128)S(1)} %collective-permute-done.2, bf16[1,128,1536]{2,1,0:T(8,128)(2,1)S(1)} %copy-done.11, f32[1536]{0:T(1024)S(1)} %get-tuple-element.265, ...), kind=kLoop, calls=%fused_computation.100 | loop fusion | flops 18874368 | bytes 1947776 | tf_op jit(solution)/shard_map/convert_element_type | solution.py:151
  107.2 2.9 fusion.130
  111.1 2.1 reshape.121
  115.5 6.7 %all-to-all-start.4 = ((bf16[8,128,96]{1,2,0:T(8,128)(2,1)}), bf16[8,128,96]{1,2,0:T(8,128)(2,1)S(1)}, u32[]{:S(2)}, u32[]{:S(2)}) async-start(bf16[8,128,96]{1,2,0:T(8,128)(2,1)} %bitcast.121), calls=%async_computation.4 | async-start | bytes 393216 | tf_op jit(solution)/shard_map/all_to_all | solution.py:157
  122.4 3.0 multiply_reduce_fusion.18
  128.9 3.5 %stack.127 = f32[31,1536]{1,0:T(8,128)} concatenate(f32[1,1536]{1,0:T(1,128)} %stack.96, f32[1,1536]{1,0:T(1,128)} %stack.97, f32[1,1536]{1,0:T(1,128)} %stack.98, f32[1,1536]{1,0:T(1,128)} %stack.99, f32[1,1536]{1,0:T(1,128)} %stack.100, f32[1,1536]{1,0:T(1,128)S(1)} %stack.101, f32[1,1536]{1,0:T(1,128)S(1)} %stack.102, f32[1,1536]{1,0:T(1,128)S(1)} %stack.103, ...), dimensions={0} | concatenate | bytes 380928 | tf_op jit(solution)/shard_map/stack | solution.py:142
  136.5 12.9 %while.25 = (s32[]{:T(128)}, bf16[2,512,96]{1,2,0:T(8,128)(2,1)}, bf16[2,512,96]{2,1,0:T(8,128)(2,1)S(1)}, bf16[1024,96]{1,0:T(8,128)(2,1)S(1)}, f32[2,512]{1,0:...) while((s32[]{:T(128)}, bf16[2,512,96]{1,2,0:T(8,128)(2,1)}, ...), condition=%wide.region_6.7_spmd.clone, body=%wide.region_5.6_spmd.clone.sunk | while | flops 305185792 | bytes 6241429 | solution.py:73
  139.8 3.3 %fusion.163 = bf16[2,512,96]{1,2,0:T(8,128)(2,1)} fusion(bf16[2,512,96]{1,2,0:T(8,128)(2,1)} %get-tuple-element.455, s32[]{:T(128)S(6)} %copy.133, bf16[1024,96]{1,0:T(8,128)(2,1)S(1)} %get-tuple-element.467, f32[512,1024]{1,0:T(8,128)} %fusion.162, bf16[1024,96]{1,0:T(8,128)(2,1)S(1)} %get-tuple-element.470, f32[512]{0:T(512)S(1)} %bitcast.129, ...), kind=kOutput, calls=%fused_computation.17.clone.1 | convolution fusion | flops 204521472 | bytes 2955264 | tf_op jit(solution)/shard_map/while/body/eval_jaxpr/dot_general | solution.py:71
  146.2 3.2 fusion.163
  151.3 2.7 reshape.123
  154.0 3.7 %reduce.64 = bf16[1024,96]{1,0:T(8,128)(2,1)} reduce(bf16[1024,1,96]{2,1,0:T(2,128)(2,1)} %bitcast.116, bf16[]{:T(256)} %broadcast.73), dimensions={1}, to_apply=%bitcast.68.reduce_sub_computation | reduce | bytes 393218
  159.8 4.5 %all-to-all-start.5 = ((bf16[8,2,6144]{2,1,0:T(2,128)(2,1)}), bf16[8,2,6144]{2,1,0:T(2,128)(2,1)}, u32[]{:S(2)}, u32[]{:S(2)}) async-start(bf16[8,2,6144]{2,1,0:T(2,128)(2,1)} %reshape.157), calls=%async_computation.5 | async-start | bytes 393216 | tf_op jit(solution)/shard_map/all_to_all | solution.py:165
  164.3 48.2 %reduce-scatter.2.cloned.1.call-done = f32[192,768]{1,0:T(8,128)} async-done(((f32[1536,768]{1,0:T(8,128)}), f32[192,768]{1,0:T(8,128)}) %reduce-scatter.2.cloned.1.call-update) | async-done | bytes 589840 | tf_op jit(solution)/shard_map/reduce_scatter | solution.py:170
  215.4 40.3 %psum.23 = f32[1536]{0:T(1024)S(1)} all-reduce(f32[1536]{0:T(1024)S(1)} %copy-done.48), channel_id=1, replica_groups=mesh['seq'=8,'dp'=4] {'seq','dp'}, use_global_device_ids=true, to_apply=%region_42.43 | all-reduce | flops 1536 | bytes 12288 | tf_op jit(solution)/shard_map/psum | solution.py:172
  256.4 20.2 %all-reduce.5.cloned.1.call-done = f32[31,1536]{1,0:T(8,128)} async-done(((f32[31,1536]{1,0:T(8,128)}), f32[31,1536]{1,0:T(8,128)}) %all-reduce.5.cloned.1.call-update) | async-done | bytes 190480 | tf_op jit(solution)/shard_map/psum | solution.py:172
  280.6 31.7 %all-reduce.3.cloned.1.call-done = bf16[192,768]{1,0:T(8,128)(2,1)} async-done(((bf16[192,768]{1,0:T(8,128)(2,1)}), bf16[192,768]{1,0:T(8,128)(2,1)}) %all-reduce.3.cloned.1.call-update) | async-done | bytes 294928 | tf_op jit(solution)/shard_map/psum | solution.py:171
  (210 shorter events, 56.5 us)
Async XLA Ops:
  8.0 67.7 %copy-start = (bf16[1536,768]{1,0:T(8,128)(2,1)S(1)}, bf16[1536,768]{1,0:T(8,128)(2,1)}, u32[]{:S(2)}) copy-start(bf16[1536,768]{1,0:T(8,128)(2,1)} %param.18) | copy-start | bytes 7077892
  9.9 15.2 %all-to-all-start = ((bf16[8,128,96]{1,2,0:T(8,128)(2,1)}), bf16[8,128,96]{1,2,0:T(8,128)(2,1)S(1)}, u32[]{:S(2)}, u32[]{:S(2)}) async-start(bf16[8,128,96]{1,2,0:T(8,128)(2,1)} %bitcast.3), calls=%async_computation | async-start | bytes 393216 | tf_op jit(solution)/shard_map/all_to_all | solution.py:107
  25.1 11.1 %all-to-all-start.1 = ((bf16[8,128,96]{1,2,0:T(8,128)(2,1)}), bf16[8,128,96]{1,2,0:T(8,128)(2,1)S(1)}, u32[]{:S(2)}, u32[]{:S(2)}) async-start(bf16[8,128,96]{1,2,0:T(8,128)(2,1)} %bitcast.5), calls=%async_computation.1 | async-start | bytes 393216 | tf_op jit(solution)/shard_map/all_to_all | solution.py:117
  36.3 11.1 %all-to-all-start.2 = ((bf16[8,128,96]{1,2,0:T(8,128)(2,1)}), bf16[8,128,96]{1,2,0:T(8,128)(2,1)S(1)}, u32[]{:S(2)}, u32[]{:S(2)}) async-start(bf16[8,128,96]{1,2,0:T(8,128)(2,1)} %bitcast.7), calls=%async_computation.2 | async-start | bytes 393216 | tf_op jit(solution)/shard_map/all_to_all | solution.py:118
  52.2 14.0 %copy-start.49 = (f32[2,512]{1,0:T(2,128)}, f32[2,512]{1,0:T(2,128)S(1)}, u32[]{:S(2)}) copy-start(f32[2,512]{1,0:T(2,128)S(1)} %get-tuple-element.448) | copy-start | bytes 12292
  52.3 23.3 %copy-start.1 = (bf16[1024,96]{1,0:T(8,128)(2,1)}, bf16[1024,96]{1,0:T(8,128)(2,1)S(1)}, u32[]{:S(2)}) copy-start(bf16[1024,96]{1,0:T(8,128)(2,1)S(1)} %get-tuple-element.477) | copy-start | bytes 589828
  52.3 23.3 %copy-start.3 = (bf16[1024,96]{1,0:T(8,128)(2,1)}, bf16[1024,96]{1,0:T(8,128)(2,1)S(1)}, u32[]{:S(2)}) copy-start(bf16[1024,96]{1,0:T(8,128)(2,1)S(1)} %get-tuple-element.480) | copy-start | bytes 589828
  52.3 23.3 %copy-start.5 = (bf16[2,512,96]{2,1,0:T(8,128)(2,1)}, bf16[2,512,96]{2,1,0:T(8,128)(2,1)S(1)}, u32[]{:S(2)}) copy-start(bf16[2,512,96]{2,1,0:T(8,128)(2,1)S(1)} %get-tuple-element.481) | copy-start | bytes 589828
  62.1 11.1 %all-to-all-start.3 = ((bf16[8,2,6144]{2,1,0:T(2,128)(2,1)}), bf16[8,2,6144]{2,1,0:T(2,128)(2,1)S(1)}, u32[]{:S(2)}, u32[]{:S(2)}) async-start(bf16[8,2,6144]{2,1,0:T(2,128)(2,1)} %reshape.155), calls=%async_computation.3 | async-start | bytes 393216 | tf_op jit(solution)/shard_map/all_to_all | solution.py:125
  65.5 147.0 %reduce-scatter.2.cloned.1.call-start = ((), (), s32[]{:S(2)}) async-start(), calls=%async_computation.7 | async-start | bytes 5308416 | tf_op jit(solution)/shard_map/reduce_scatter | solution.py:170
  75.7 11.0 %copy-start.11 = (bf16[1,128,1536]{2,1,0:T(8,128)(2,1)S(1)}, bf16[1,128,1536]{2,1,0:T(8,128)(2,1)}, u32[]{:S(2)}) copy-start(bf16[1,128,1536]{2,1,0:T(8,128)(2,1)} %param.21) | copy-start | bytes 1179652
  75.7 11.0 %copy-start.13 = (f32[1536]{0:T(1024)S(1)}, f32[1536]{0:T(1024)}, u32[]{:S(2)}) copy-start(f32[1536]{0:T(1024)} %get-tuple-element.238) | copy-start | bytes 18436
  75.7 11.0 %copy-start.14 = (f32[1536]{0:T(1024)S(1)}, f32[1536]{0:T(1024)}, u32[]{:S(2)}) copy-start(f32[1536]{0:T(1024)} %get-tuple-element.239) | copy-start | bytes 18436
  75.7 11.0 %copy-start.15 = (f32[1536]{0:T(1024)S(1)}, f32[1536]{0:T(1024)}, u32[]{:S(2)}) copy-start(f32[1536]{0:T(1024)} %get-tuple-element.240) | copy-start | bytes 18436
  75.7 11.0 %copy-start.16 = (f32[1536]{0:T(1024)S(1)}, f32[1536]{0:T(1024)}, u32[]{:S(2)}) copy-start(f32[1536]{0:T(1024)} %get-tuple-element.241) | copy-start | bytes 18436
  75.7 11.0 %copy-start.17 = (f32[1536]{0:T(1024)S(1)}, f32[1536]{0:T(1024)}, u32[]{:S(2)}) copy-start(f32[1536]{0:T(1024)} %get-tuple-element.242) | copy-start | bytes 18436
  75.7 11.0 %copy-start.18 = (f32[1536]{0:T(1024)S(1)}, f32[1536]{0:T(1024)}, u32[]{:S(2)}) copy-start(f32[1536]{0:T(1024)} %get-tuple-element.243) | copy-start | bytes 18436
  78.6 4.9 %collective-permute-start = (bf16[15,1536]{1,0:T(8,128)(2,1)S(1)}, bf16[15,1536]{1,0:T(8,128)(2,1)S(1)}, u32[]{:S(2)}, u32[]{:S(2)}) collective-permute-start(bf16[15,1536]{1,0:T(8,128)(2,1)S(1)} %get-tuple-element.307), channel_id=1, source_target_pairs={{0,4},{4,8},{8,12},{12,16},{16,20},{20,24},{24,28},{1,5},{5,9},{9,... | collective-permute-start | bytes 138248 | tf_op jit(solution)/shard_map/ppermute | solution.py:21
  80.6 6.0 %collective-permute-start.1 = (bf16[15,1536]{1,0:T(8,128)(2,1)S(1)}, bf16[15,1536]{1,0:T(8,128)(2,1)S(1)}, u32[]{:S(2)}, u32[]{:S(2)}) collective-permute-start(bf16[15,1536]{1,0:T(8,128)(2,1)S(1)} %get-tuple-element.308), channel_id=1, source_target_pairs={{4,0},{8,4},{12,8},{16,12},{20,16},{24,20},{28,24},{5,1},{9,5},{13... | collective-permute-start | bytes 138248 | tf_op jit(solution)/shard_map/ppermute | solution.py:22
  94.4 6.7 %collective-permute-start.2 = (f32[15,1536]{1,0:T(8,128)S(1)}, f32[15,1536]{1,0:T(8,128)S(1)}, u32[]{:S(2)}, u32[]{:S(2)}) collective-permute-start(f32[15,1536]{1,0:T(8,128)S(1)} %get-tuple-element.305), channel_id=1, source_target_pairs={{4,0},{8,4},{12,8},{16,12},{20,16},{24,20},{28,24},{5,1},{9,5},{13... | collective-permute-start | bytes 276488 | tf_op jit(solution)/shard_map/ppermute | solution.py:22
  95.7 7.0 %collective-permute-start.3 = (f32[15,1536]{1,0:T(8,128)S(1)}, f32[15,1536]{1,0:T(8,128)S(1)}, u32[]{:S(2)}, u32[]{:S(2)}) collective-permute-start(f32[15,1536]{1,0:T(8,128)S(1)} %get-tuple-element.306), channel_id=1, source_target_pairs={{0,4},{4,8},{8,12},{12,16},{16,20},{20,24},{24,28},{1,5},{5,9},{9,... | collective-permute-start | bytes 276488 | tf_op jit(solution)/shard_map/ppermute | solution.py:21
  115.5 18.4 %all-to-all-start.4 = ((bf16[8,128,96]{1,2,0:T(8,128)(2,1)}), bf16[8,128,96]{1,2,0:T(8,128)(2,1)S(1)}, u32[]{:S(2)}, u32[]{:S(2)}) async-start(bf16[8,128,96]{1,2,0:T(8,128)(2,1)} %bitcast.121), calls=%async_computation.4 | async-start | bytes 393216 | tf_op jit(solution)/shard_map/all_to_all | solution.py:157
  122.2 154.4 %all-reduce.5.cloned.1.call-start = ((), (), s32[]{:S(2)}) async-start(), calls=%async_computation.9 | async-start | bytes 393216 | tf_op jit(solution)/shard_map/psum | solution.py:172
  125.4 11.2 %copy-start.2 = (bf16[1024,96]{1,0:T(8,128)(2,1)S(1)}, bf16[1024,96]{1,0:T(8,128)(2,1)}, u32[]{:S(2)}) copy-start(bf16[1024,96]{1,0:T(8,128)(2,1)} %copy-done.1) | copy-start | bytes 589828
  125.4 11.2 %copy-start.4 = (bf16[1024,96]{1,0:T(8,128)(2,1)S(1)}, bf16[1024,96]{1,0:T(8,128)(2,1)}, u32[]{:S(2)}) copy-start(bf16[1024,96]{1,0:T(8,128)(2,1)} %copy-done.3) | copy-start | bytes 589828
  125.4 11.2 %copy-start.6 = (bf16[2,512,96]{2,1,0:T(8,128)(2,1)S(1)}, bf16[2,512,96]{2,1,0:T(8,128)(2,1)}, u32[]{:S(2)}) copy-start(bf16[2,512,96]{2,1,0:T(8,128)(2,1)} %copy-done.5) | copy-start | bytes 589828
  149.4 64.9 %copy-start.9 = (f32[128,1536]{1,0:T(8,128)S(1)}, f32[128,1536]{1,0:T(8,128)}, u32[]{:S(2)}) copy-start(f32[128,1536]{1,0:T(8,128)} %get-tuple-element.300) | copy-start | bytes 2359300
  149.5 64.9 %copy-start.10 = (bf16[128,1536]{1,0:T(8,128)(2,1)S(1)}, bf16[128,1536]{1,0:T(8,128)(2,1)}, u32[]{:S(2)}) copy-start(bf16[128,1536]{1,0:T(8,128)(2,1)} %get-tuple-element.310) | copy-start | bytes 1179652
  149.5 64.9 %copy-start.51 = (pred[128]{0:T(512)(128)(4,1)S(1)}, pred[128]{0:T(512)(128)(4,1)}, u32[]{:S(2)}) copy-start(pred[128]{0:T(512)(128)(4,1)} %add_compare_fusion) | copy-start | bytes 388
  154.0 61.4 %copy-start.48 = (f32[1536]{0:T(1024)S(1)}, f32[1536]{0:T(1024)}, u32[]{:S(2)}) copy-start(f32[1536]{0:T(1024)} %get-tuple-element.235) | copy-start | bytes 18436
  159.8 118.3 %all-to-all-start.5 = ((bf16[8,2,6144]{2,1,0:T(2,128)(2,1)}), bf16[8,2,6144]{2,1,0:T(2,128)(2,1)}, u32[]{:S(2)}, u32[]{:S(2)}) async-start(bf16[8,2,6144]{2,1,0:T(2,128)(2,1)} %reshape.157), calls=%async_computation.5 | async-start | bytes 393216 | tf_op jit(solution)/shard_map/all_to_all | solution.py:165
  164.2 148.0 %all-reduce.3.cloned.1.call-start = ((), (), s32[]{:S(2)}) async-start(), calls=%async_computation.8 | async-start | bytes 589824 | tf_op jit(solution)/shard_map/psum | solution.py:171
  (35 other events, 218.9 us)
Sparse Core Ops, SparseCore 0:
  110.3 102.1 reduce-scatter.1
Sparse Core Ops, SparseCore 1:
  132.5 144.0 all-reduce.4
  279.3 32.9 all-reduce.2
where the time goes:
time: 324 us; the launch traced here: 322 us
  waiting for transfers between devices  130 us (40%)
  local copies, waits for them, and re-layouts  44.2 us (14%)
  blocking collectives  40.3 us (12%)
  starting transfers between devices  38.2 us (12%)
  other arithmetic  31.9 us (10%)
  matrix products  19.4 us (6%)
  between operations  17.3 us (5%)
    reduce_scatter x1, waiting for transfers between devices, on_device(): lax.psum_scatter(term_block, 'seq', scatter_dimension=0, tiled=True)  48.2 us
    psum x1, blocking collectives, on_device(): lax.psum((kernel_local, bias_local), ('seq', 'dp'))  40.3 us
    psum x1, waiting for transfers between devices, on_device(): lax.psum(partial_rows.astype(jnp.bfloat16), 'dp').astype(jnp.float32)  31.7 us
    psum x1, waiting for transfers between devices, on_device(): lax.psum((kernel_local, bias_local), ('seq', 'dp'))  20.2 us
    unnamed x119, local copies, waits for them, and re-layouts  15.6 us
    reduce_sum x2, other arithmetic, on_device(): jnp.sum(grad_conv * padded[tap:tap + frames_dev], axis=0)  10.5 us
    unnamed x2, other arithmetic  7.45 us
    all_to_all x1, waiting for transfers between devices, on_device(): lax.all_to_all(value_send, 'seq', split_axis=0, concat_axis=1, tiled=True)  7.34 us
  transfers between devices with their start and end apart: 13, of which 11 were waited for; matrix products, arithmetic and copies ran while one was open for 18% of the time, Pallas kernels for 0%

commit v1 on v0

--- a/solution.py
+++ b/solution.py
@@ -9,6 +9,22 @@
 HS = 96
 KW = 31
 HD = 768
+
+
+def exchange_in_pairs(x, axis, split, join):
+    ways, here = (lax.axis_size(axis), lax.axis_index(axis))
+    width = x.shape[split] // ways
+    lengths = list(x.shape)
+    lengths[split] = width
+    height = lengths[join]
+    lengths[join] = height * ways
+    full = jnp.zeros(lengths, x.dtype)
+    for mask in range(ways):
+        part = lax.dynamic_slice_in_dim(x, (here ^ mask) * width, width, axis=split)
+        if mask:
+            part = lax.ppermute(part, axis, [(d, d ^ mask) for d in range(ways)])
+        full = lax.dynamic_update_slice_in_dim(full, part, (here ^ mask) * height, axis=join)
+    return full
 
 
 def with_halo(x, sides, width):
@@ -115,7 +131,7 @@
     )
     key_mine, value_mine = (
         lax.all_to_all(key_send, "seq", split_axis=0, concat_axis=1, tiled=True),
-        lax.all_to_all(value_send, "seq", split_axis=0, concat_axis=1, tiled=True),
+        exchange_in_pairs(value_send, "seq", 0, 1),
     )
     key_mine = key_mine[0]
     value_mine = value_mine[0]

time: 324 us -> 321 us (level)
  waiting for transfers between devices: 130 us -> 118 us
  starting transfers between devices: 38.2 us -> 47.7 us
    ppermute x0 -> x7, starting transfers between devices: none -> 11.1 us  [exchange_in_pairs(): part = lax.ppermute(part, axis, [(d, d ^ mask) for d in range(ways)])]
    all_to_all x1 -> x0, waiting for transfers between devices: 7.34 us -> none  [on_device(): lax.all_to_all(value_send, 'seq', split_axis=0, concat_axis=1, tiled=True)]
    all_to_all x1, waiting for transfers between devices: 6.21 us -> 0.01 us  [on_device(): lax.all_to_all(to_serving(query_local), 'seq', split_axis=0, concat_axis=...]
    all_to_all x1 -> x0, starting transfers between devices: 3.39 us -> none  [on_device(): lax.all_to_all(value_send, 'seq', split_axis=0, concat_axis=1, tiled=True)]
    unnamed x119 -> x120, local copies, waits for them, and re-layouts: 15.6 us -> 13.9 us
  transfers between devices with their start and end apart: 13 -> 19, of which waited for: 11 -> 10; matrix products, arithmetic and copies ran while one was open for 18% -> 18% of each run, Pallas kernels for 0% -> 0%
where the time goes in v1:
time: 321 us; the launch traced here: 319 us
  waiting for transfers between devices  118 us (37%)
  starting transfers between devices  47.7 us (15%)
  local copies, waits for them, and re-layouts  43.6 us (14%)
  blocking collectives  40.3 us (13%)
  other arithmetic  31.9 us (10%)
  matrix products  19.4 us (6%)
  between operations  17.5 us (5%)
    reduce_scatter x1, waiting for transfers between devices, on_device(): lax.psum_scatter(term_block, 'seq', scatter_dimension=0, tiled=True)  48.5 us
    psum x1, blocking collectives, on_device(): lax.psum((kernel_local, bias_local), ('seq', 'dp'))  40.3 us
    psum x1, waiting for transfers between devices, on_device(): lax.psum(partial_rows.astype(jnp.bfloat16), 'dp').astype(jnp.float32)  31.7 us
    psum x1, waiting for transfers between devices, on_device(): lax.psum((kernel_local, bias_local), ('seq', 'dp'))  20.2 us
    unnamed x120, local copies, waits for them, and re-layouts  13.9 us
    ppermute x7, starting transfers between devices, exchange_in_pairs(): part = lax.ppermute(part, axis, [(d, d ^ mask) for d in range(ways)])  11.1 us
    reduce_sum x2, other arithmetic, on_device(): jnp.sum(grad_conv * padded[tap:tap + frames_dev], axis=0)  10.5 us
    unnamed x2, other arithmetic  7.45 us
  transfers between devices with their start and end apart: 19, of which 10 were waited for; matrix products, arithmetic and copies ran while one was open for 18% of the time, Pallas kernels for 0%

profile of v1, /device:TPU:0, one launch (start us, length us, event | category | flops | bytes accessed | tf_op | source)
XLA Modules:
  0.0 318.7 jit_solution(5850538898889827878)
XLA Ops:
  9.9 7.3 %all-to-all-start = ((bf16[8,128,96]{1,2,0:T(8,128)(2,1)}), bf16[8,128,96]{1,2,0:T(8,128)(2,1)S(1)}, u32[]{:S(2)}, u32[]{:S(2)}) async-start(bf16[8,128,96]{1,2,0:T(8,128)(2,1)} %bitcast.3), calls=%async_computation | async-start | bytes 393216 | tf_op jit(solution)/shard_map/all_to_all | solution.py:123
  18.4 4.8 %collective-permute-start.6 = (bf16[1,128,96]{1,2,0:T(8,128)(2,1)S(1)}, bf16[1,128,96]{1,2,0:T(8,128)(2,1)S(1)}, u32[]{:S(2)}, u32[]{:S(2)}) collective-permute-start(bf16[1,128,96]{1,2,0:T(8,128)(2,1)S(1)} %get-tuple-element.309), channel_id=1, source_target_pairs={{0,28},{4,24},{8,20},{12,16},{16,12},{20,8},{24,4},{28,0},{1,29},{... | collective-permute-start | bytes 73736 | tf_op jit(solution)/shard_map/ppermute | solution.py:25
  27.9 2.2 collective-permute-start.5
  31.3 5.1 %all-to-all-start.1 = ((bf16[8,128,96]{1,2,0:T(8,128)(2,1)}), bf16[8,128,96]{1,2,0:T(8,128)(2,1)S(1)}, u32[]{:S(2)}, u32[]{:S(2)}) async-start(bf16[8,128,96]{1,2,0:T(8,128)(2,1)} %bitcast.5), calls=%async_computation.1 | async-start | bytes 393216 | tf_op jit(solution)/shard_map/all_to_all | solution.py:133
  37.0 7.1 %all-to-all-done.1 = bf16[8,128,96]{1,2,0:T(8,128)(2,1)S(1)} async-done(((bf16[8,128,96]{1,2,0:T(8,128)(2,1)}), bf16[8,128,96]{1,2,0:T(8,128)(2,1)S(1)}, u32[]{:S(2)}, u32[]{:S(2)}) %all-to-all-start.1) | async-done | bytes 196640 | tf_op jit(solution)/shard_map/all_to_all | solution.py:133
  44.4 4.6 %while.24 = (s32[]{:T(128)}, bf16[2,512,96]{1,2,0:T(8,128)(2,1)S(1)}, f32[2,512]{1,0:T(2,128)S(1)}, bf16[2,512,96]{2,1,0:T(8,128)(2,1)S(1)}, bf16[1024,96]{1,0:T...) while((s32[]{:T(128)}, ...), condition=%wide.region_3.4_spmd.clone, body=%wide.region_0.3_spmd.clone.sunk | while | flops 204997120 | bytes 7164021 | solution.py:61
  50.0 2.6 reshape.143
  53.1 3.7 %reduce.63 = bf16[1024,96]{1,0:T(8,128)(2,1)} reduce(bf16[1024,1,96]{2,1,0:T(2,128)(2,1)} %bitcast.134, bf16[]{:T(256)} %broadcast.75), dimensions={1}, to_apply=%bitcast.86.reduce_sub_computation | reduce | bytes 393218
  58.9 3.4 %all-to-all-start.2 = ((bf16[8,2,6144]{2,1,0:T(2,128)(2,1)}), bf16[8,2,6144]{2,1,0:T(2,128)(2,1)S(1)}, u32[]{:S(2)}, u32[]{:S(2)}) async-start(bf16[8,2,6144]{2,1,0:T(2,128)(2,1)} %reshape.176), calls=%async_computation.2 | async-start | bytes 393216 | tf_op jit(solution)/shard_map/all_to_all | solution.py:141
  63.6 2.5 slice_reduce_fusion.30
  66.1 3.9 %all-to-all-done.2 = bf16[8,2,6144]{2,1,0:T(2,128)(2,1)S(1)} async-done(((bf16[8,2,6144]{2,1,0:T(2,128)(2,1)}), bf16[8,2,6144]{2,1,0:T(2,128)(2,1)S(1)}, u32[]{:S(2)}, u32[]{:S(2)}) %all-to-all-start.2) | async-done | bytes 196640 | tf_op jit(solution)/shard_map/all_to_all | solution.py:141
  72.7 2.7 broadcast_select_fusion
  80.3 3.0 collective-permute-done.8
  83.7 7.5 %multiply_reduce_fusion = (f32[1536]{0:T(1024)}, f32[1536]{0:T(1024)}, f32[1536]{0:T(1024)}, f32[1536]{0:T(1024)}, f32[1536]{0:T(1024)}, /*index=5*/f32[1536]{0:...) fusion(f32[158,1536]{1,0:T(8,128)S(1)} %maximum_convert_fusion,, ...), kind=kLoop, calls=%fused_computation.190 | loop fusion | flops 21206016 | bytes 26652800 | tf_op jit(solution)/shard_map/reduce_sum | solution.py:159
  92.5 5.0 %collective-permute-start.10 = (f32[15,1536]{1,0:T(8,128)S(1)}, f32[15,1536]{1,0:T(8,128)S(1)}, u32[]{:S(2)}, u32[]{:S(2)}) collective-permute-start(f32[15,1536]{1,0:T(8,128)S(1)} %get-tuple-element.306), channel_id=1, source_target_pairs={{0,4},{4,8},{8,12},{12,16},{16,20},{20,24},{24,28},{1,5},{5,9},{9,... | collective-permute-start | bytes 276488 | tf_op jit(solution)/shard_map/ppermute | solution.py:37
  99.5 3.7 %fusion.37 = bf16[128,1536]{1,0:T(8,128)(2,1)S(1)} fusion(f32[128,1536]{1,0:T(8,128)S(1)} %get-tuple-element.299, f32[15,1536]{1,0:T(8,128)S(1)} %collective-permute-done.10, f32[15,1536]{1,0:T(8,128)S(1)} %collective-permute-done.9, bf16[1,128,1536]{2,1,0:T(8,128)(2,1)S(1)} %copy-done.11, f32[1536]{0:T(1024)S(1)} %get-tuple-element.265, ...), kind=kLoop, calls=%fused_computation.100 | loop fusion | flops 18874368 | bytes 1947776 | tf_op jit(solution)/shard_map/convert_element_type | solution.py:167
  104.0 2.9 fusion.130
  107.9 2.1 reshape.142
  112.3 6.7 %all-to-all-start.3 = ((bf16[8,128,96]{1,2,0:T(8,128)(2,1)}), bf16[8,128,96]{1,2,0:T(8,128)(2,1)S(1)}, u32[]{:S(2)}, u32[]{:S(2)}) async-start(bf16[8,128,96]{1,2,0:T(8,128)(2,1)} %bitcast.140), calls=%async_computation.3 | async-start | bytes 393216 | tf_op jit(solution)/shard_map/all_to_all | solution.py:173
  119.2 3.0 multiply_reduce_fusion.18
  125.7 3.5 %stack.127 = f32[31,1536]{1,0:T(8,128)} concatenate(f32[1,1536]{1,0:T(1,128)} %stack.96, f32[1,1536]{1,0:T(1,128)} %stack.97, f32[1,1536]{1,0:T(1,128)} %stack.98, f32[1,1536]{1,0:T(1,128)} %stack.99, f32[1,1536]{1,0:T(1,128)} %stack.100, f32[1,1536]{1,0:T(1,128)S(1)} %stack.101, f32[1,1536]{1,0:T(1,128)S(1)} %stack.102, f32[1,1536]{1,0:T(1,128)S(1)} %stack.103, ...), dimensions={0} | concatenate | bytes 380928 | tf_op jit(solution)/shard_map/stack | solution.py:158
  133.3 12.9 %while.25 = (s32[]{:T(128)}, bf16[2,512,96]{1,2,0:T(8,128)(2,1)}, bf16[2,512,96]{2,1,0:T(8,128)(2,1)S(1)}, bf16[1024,96]{1,0:T(8,128)(2,1)S(1)}, f32[2,512]{1,0:...) while((s32[]{:T(128)}, bf16[2,512,96]{1,2,0:T(8,128)(2,1)}, ...), condition=%wide.region_6.7_spmd.clone, body=%wide.region_5.6_spmd.clone.sunk | while | flops 305185792 | bytes 6241429 | solution.py:89
  136.6 3.3 %fusion.163 = bf16[2,512,96]{1,2,0:T(8,128)(2,1)} fusion(bf16[2,512,96]{1,2,0:T(8,128)(2,1)} %get-tuple-element.463, s32[]{:T(128)S(6)} %copy.161, bf16[1024,96]{1,0:T(8,128)(2,1)S(1)} %get-tuple-element.475, f32[512,1024]{1,0:T(8,128)} %fusion.162, bf16[1024,96]{1,0:T(8,128)(2,1)S(1)} %get-tuple-element.478, f32[512]{0:T(512)S(1)} %bitcast.149, ...), kind=kOutput, calls=%fused_computation.17.clone.1 | convolution fusion | flops 204521472 | bytes 2955264 | tf_op jit(solution)/shard_map/while/body/eval_jaxpr/dot_general | solution.py:87
  143.0 3.2 %fusion.163 = bf16[2,512,96]{1,2,0:T(8,128)(2,1)} fusion(bf16[2,512,96]{1,2,0:T(8,128)(2,1)} %get-tuple-element.463, s32[]{:T(128)S(6)} %copy.161, bf16[1024,96]{1,0:T(8,128)(2,1)S(1)} %get-tuple-element.475, f32[512,1024]{1,0:T(8,128)} %fusion.162, bf16[1024,96]{1,0:T(8,128)(2,1)S(1)} %get-tuple-element.478, f32[512]{0:T(512)S(1)} %bitcast.149, ...), kind=kOutput, calls=%fused_computation.17.clone.1 | convolution fusion | flops 204521472 | bytes 2955264 | tf_op jit(solution)/shard_map/while/body/eval_jaxpr/dot_general | solution.py:87
  148.1 2.6 reshape.144
  150.8 3.7 %reduce.64 = bf16[1024,96]{1,0:T(8,128)(2,1)} reduce(bf16[1024,1,96]{2,1,0:T(2,128)(2,1)} %bitcast.135, bf16[]{:T(256)} %broadcast.75), dimensions={1}, to_apply=%bitcast.88.reduce_sub_computation | reduce | bytes 393218
  154.5 2.1 reshape.178
  156.6 4.5 %all-to-all-start.4 = ((bf16[8,2,6144]{2,1,0:T(2,128)(2,1)}), bf16[8,2,6144]{2,1,0:T(2,128)(2,1)}, u32[]{:S(2)}, u32[]{:S(2)}) async-start(bf16[8,2,6144]{2,1,0:T(2,128)(2,1)} %reshape.178), calls=%async_computation.4 | async-start | bytes 393216 | tf_op jit(solution)/shard_map/all_to_all | solution.py:181
  161.1 48.5 %reduce-scatter.2.cloned.1.call-done = f32[192,768]{1,0:T(8,128)} async-done(((f32[1536,768]{1,0:T(8,128)}), f32[192,768]{1,0:T(8,128)}) %reduce-scatter.2.cloned.1.call-update) | async-done | bytes 589840 | tf_op jit(solution)/shard_map/reduce_scatter | solution.py:186
  212.6 40.3 %psum.23 = f32[1536]{0:T(1024)S(1)} all-reduce(f32[1536]{0:T(1024)S(1)} %copy-done.49), channel_id=1, replica_groups=mesh['seq'=8,'dp'=4] {'seq','dp'}, use_global_device_ids=true, to_apply=%region_42.43 | all-reduce | flops 1536 | bytes 12288 | tf_op jit(solution)/shard_map/psum | solution.py:188
  253.5 20.2 %all-reduce.5.cloned.1.call-done = f32[31,1536]{1,0:T(8,128)} async-done(((f32[31,1536]{1,0:T(8,128)}), f32[31,1536]{1,0:T(8,128)}) %all-reduce.5.cloned.1.call-update) | async-done | bytes 190480 | tf_op jit(solution)/shard_map/psum | solution.py:188
  277.7 31.7 %all-reduce.3.cloned.1.call-done = bf16[192,768]{1,0:T(8,128)(2,1)} async-done(((bf16[192,768]{1,0:T(8,128)(2,1)}), bf16[192,768]{1,0:T(8,128)(2,1)}) %all-reduce.3.cloned.1.call-update) | async-done | bytes 294928 | tf_op jit(solution)/shard_map/psum | solution.py:187
  (241 shorter events, 58.0 us)
Async XLA Ops:
  8.0 64.5 %copy-start = (bf16[1536,768]{1,0:T(8,128)(2,1)S(1)}, bf16[1536,768]{1,0:T(8,128)(2,1)}, u32[]{:S(2)}) copy-start(bf16[1536,768]{1,0:T(8,128)(2,1)} %param.18) | copy-start | bytes 7077892
  8.0 18.9 %copy-start.13 = (bf16[1,128,768]{2,1,0:T(8,128)(2,1)S(1)}, bf16[1,128,768]{2,1,0:T(8,128)(2,1)}, u32[]{:S(2)}) copy-start(bf16[1,128,768]{2,1,0:T(8,128)(2,1)} %param.15) | copy-start | bytes 589828
  9.9 21.4 %all-to-all-start = ((bf16[8,128,96]{1,2,0:T(8,128)(2,1)}), bf16[8,128,96]{1,2,0:T(8,128)(2,1)S(1)}, u32[]{:S(2)}, u32[]{:S(2)}) async-start(bf16[8,128,96]{1,2,0:T(8,128)(2,1)} %bitcast.3), calls=%async_computation | async-start | bytes 393216 | tf_op jit(solution)/shard_map/all_to_all | solution.py:123
  18.4 18.0 %collective-permute-start.6 = (bf16[1,128,96]{1,2,0:T(8,128)(2,1)S(1)}, bf16[1,128,96]{1,2,0:T(8,128)(2,1)S(1)}, u32[]{:S(2)}, u32[]{:S(2)}) collective-permute-start(bf16[1,128,96]{1,2,0:T(8,128)(2,1)S(1)} %get-tuple-element.309), channel_id=1, source_target_pairs={{0,28},{4,24},{8,20},{12,16},{16,12},{20,8},{24,4},{28,0},{1,29},{... | collective-permute-start | bytes 73736 | tf_op jit(solution)/shard_map/ppermute | solution.py:25
  23.2 4.7 %collective-permute-start.3 = (bf16[1,128,96]{1,2,0:T(8,128)(2,1)S(1)}, bf16[1,128,96]{1,2,0:T(8,128)(2,1)S(1)}, u32[]{:S(2)}, u32[]{:S(2)}) collective-permute-start(bf16[1,128,96]{1,2,0:T(8,128)(2,1)S(1)} %get-tuple-element.312), channel_id=1, source_target_pairs={{0,16},{4,20},{8,24},{12,28},{16,0},{20,4},{24,8},{28,12},{1,17},{... | collective-permute-start | bytes 73736 | tf_op jit(solution)/shard_map/ppermute | solution.py:25
  23.2 7.0 %collective-permute-start.2 = (bf16[1,128,96]{1,2,0:T(8,128)(2,1)S(1)}, bf16[1,128,96]{1,2,0:T(8,128)(2,1)S(1)}, u32[]{:S(2)}, u32[]{:S(2)}) collective-permute-start(bf16[1,128,96]{1,2,0:T(8,128)(2,1)S(1)} %get-tuple-element.313), channel_id=1, source_target_pairs={{0,12},{4,8},{8,4},{12,0},{16,28},{20,24},{24,20},{28,16},{1,13},{... | collective-permute-start | bytes 73736 | tf_op jit(solution)/shard_map/ppermute | solution.py:25
  23.8 7.2 %collective-permute-start.1 = (bf16[1,128,96]{1,2,0:T(8,128)(2,1)S(1)}, bf16[1,128,96]{1,2,0:T(8,128)(2,1)S(1)}, u32[]{:S(2)}, u32[]{:S(2)}) collective-permute-start(bf16[1,128,96]{1,2,0:T(8,128)(2,1)S(1)} %get-tuple-element.314), channel_id=1, source_target_pairs={{0,8},{4,12},{8,0},{12,4},{16,24},{20,28},{24,16},{28,20},{1,9},{5... | collective-permute-start | bytes 73736 | tf_op jit(solution)/shard_map/ppermute | solution.py:25
  25.2 5.9 %collective-permute-start = (bf16[1,128,96]{1,2,0:T(8,128)(2,1)S(1)}, bf16[1,128,96]{1,2,0:T(8,128)(2,1)S(1)}, u32[]{:S(2)}, u32[]{:S(2)}) collective-permute-start(bf16[1,128,96]{1,2,0:T(8,128)(2,1)S(1)} %get-tuple-element.315), channel_id=1, source_target_pairs={{0,4},{4,0},{8,12},{12,8},{16,20},{20,16},{24,28},{28,24},{1,5},{5... | collective-permute-start | bytes 73736 | tf_op jit(solution)/shard_map/ppermute | solution.py:25
  27.9 8.6 %collective-permute-start.5 = (bf16[1,128,96]{1,2,0:T(8,128)(2,1)S(1)}, bf16[1,128,96]{1,2,0:T(8,128)(2,1)S(1)}, u32[]{:S(2)}, u32[]{:S(2)}) collective-permute-start(bf16[1,128,96]{1,2,0:T(8,128)(2,1)S(1)} %get-tuple-element.310), channel_id=1, source_target_pairs={{0,24},{4,28},{8,16},{12,20},{16,8},{20,12},{24,0},{28,4},{1,25},{... | collective-permute-start | bytes 73736 | tf_op jit(solution)/shard_map/ppermute | solution.py:25
  30.2 6.5 %collective-permute-start.4 = (bf16[1,128,96]{1,2,0:T(8,128)(2,1)S(1)}, bf16[1,128,96]{1,2,0:T(8,128)(2,1)S(1)}, u32[]{:S(2)}, u32[]{:S(2)}) collective-permute-start(bf16[1,128,96]{1,2,0:T(8,128)(2,1)S(1)} %get-tuple-element.311), channel_id=1, source_target_pairs={{0,20},{4,16},{8,28},{12,24},{16,4},{20,0},{24,12},{28,8},{1,21},{... | collective-permute-start | bytes 73736 | tf_op jit(solution)/shard_map/ppermute | solution.py:25
  31.3 12.9 %all-to-all-start.1 = ((bf16[8,128,96]{1,2,0:T(8,128)(2,1)}), bf16[8,128,96]{1,2,0:T(8,128)(2,1)S(1)}, u32[]{:S(2)}, u32[]{:S(2)}) async-start(bf16[8,128,96]{1,2,0:T(8,128)(2,1)} %bitcast.5), calls=%async_computation.1 | async-start | bytes 393216 | tf_op jit(solution)/shard_map/all_to_all | solution.py:133
  49.0 14.0 %copy-start.50 = (f32[2,512]{1,0:T(2,128)}, f32[2,512]{1,0:T(2,128)S(1)}, u32[]{:S(2)}) copy-start(f32[2,512]{1,0:T(2,128)S(1)} %get-tuple-element.456) | copy-start | bytes 12292
  49.1 23.3 %copy-start.1 = (bf16[1024,96]{1,0:T(8,128)(2,1)}, bf16[1024,96]{1,0:T(8,128)(2,1)S(1)}, u32[]{:S(2)}) copy-start(bf16[1024,96]{1,0:T(8,128)(2,1)S(1)} %get-tuple-element.485) | copy-start | bytes 589828
  49.1 23.3 %copy-start.3 = (bf16[1024,96]{1,0:T(8,128)(2,1)}, bf16[1024,96]{1,0:T(8,128)(2,1)S(1)}, u32[]{:S(2)}) copy-start(bf16[1024,96]{1,0:T(8,128)(2,1)S(1)} %get-tuple-element.488) | copy-start | bytes 589828
  49.1 23.3 %copy-start.5 = (bf16[2,512,96]{2,1,0:T(8,128)(2,1)}, bf16[2,512,96]{2,1,0:T(8,128)(2,1)S(1)}, u32[]{:S(2)}) copy-start(bf16[2,512,96]{2,1,0:T(8,128)(2,1)S(1)} %get-tuple-element.489) | copy-start | bytes 589828
  58.9 11.1 %all-to-all-start.2 = ((bf16[8,2,6144]{2,1,0:T(2,128)(2,1)}), bf16[8,2,6144]{2,1,0:T(2,128)(2,1)S(1)}, u32[]{:S(2)}, u32[]{:S(2)}) async-start(bf16[8,2,6144]{2,1,0:T(2,128)(2,1)} %reshape.176), calls=%async_computation.2 | async-start | bytes 393216 | tf_op jit(solution)/shard_map/all_to_all | solution.py:141
  62.3 147.3 %reduce-scatter.2.cloned.1.call-start = ((), (), s32[]{:S(2)}) async-start(), calls=%async_computation.6 | async-start | bytes 5308416 | tf_op jit(solution)/shard_map/reduce_scatter | solution.py:186
  75.4 4.9 %collective-permute-start.7 = (bf16[15,1536]{1,0:T(8,128)(2,1)S(1)}, bf16[15,1536]{1,0:T(8,128)(2,1)S(1)}, u32[]{:S(2)}, u32[]{:S(2)}) collective-permute-start(bf16[15,1536]{1,0:T(8,128)(2,1)S(1)} %get-tuple-element.307), channel_id=1, source_target_pairs={{0,4},{4,8},{8,12},{12,16},{16,20},{20,24},{24,28},{1,5},{5,9},{9,... | collective-permute-start | bytes 138248 | tf_op jit(solution)/shard_map/ppermute | solution.py:37
  77.4 6.0 %collective-permute-start.8 = (bf16[15,1536]{1,0:T(8,128)(2,1)S(1)}, bf16[15,1536]{1,0:T(8,128)(2,1)S(1)}, u32[]{:S(2)}, u32[]{:S(2)}) collective-permute-start(bf16[15,1536]{1,0:T(8,128)(2,1)S(1)} %get-tuple-element.308), channel_id=1, source_target_pairs={{4,0},{8,4},{12,8},{16,12},{20,16},{24,20},{28,24},{5,1},{9,5},{13... | collective-permute-start | bytes 138248 | tf_op jit(solution)/shard_map/ppermute | solution.py:38
  91.2 6.7 %collective-permute-start.9 = (f32[15,1536]{1,0:T(8,128)S(1)}, f32[15,1536]{1,0:T(8,128)S(1)}, u32[]{:S(2)}, u32[]{:S(2)}) collective-permute-start(f32[15,1536]{1,0:T(8,128)S(1)} %get-tuple-element.305), channel_id=1, source_target_pairs={{4,0},{8,4},{12,8},{16,12},{20,16},{24,20},{28,24},{5,1},{9,5},{13... | collective-permute-start | bytes 276488 | tf_op jit(solution)/shard_map/ppermute | solution.py:38
  92.5 7.0 %collective-permute-start.10 = (f32[15,1536]{1,0:T(8,128)S(1)}, f32[15,1536]{1,0:T(8,128)S(1)}, u32[]{:S(2)}, u32[]{:S(2)}) collective-permute-start(f32[15,1536]{1,0:T(8,128)S(1)} %get-tuple-element.306), channel_id=1, source_target_pairs={{0,4},{4,8},{8,12},{12,16},{16,20},{20,24},{24,28},{1,5},{5,9},{9,... | collective-permute-start | bytes 276488 | tf_op jit(solution)/shard_map/ppermute | solution.py:37
  112.3 18.4 %all-to-all-start.3 = ((bf16[8,128,96]{1,2,0:T(8,128)(2,1)}), bf16[8,128,96]{1,2,0:T(8,128)(2,1)S(1)}, u32[]{:S(2)}, u32[]{:S(2)}) async-start(bf16[8,128,96]{1,2,0:T(8,128)(2,1)} %bitcast.140), calls=%async_computation.3 | async-start | bytes 393216 | tf_op jit(solution)/shard_map/all_to_all | solution.py:173
  119.0 154.7 %all-reduce.5.cloned.1.call-start = ((), (), s32[]{:S(2)}) async-start(), calls=%async_computation.8 | async-start | bytes 393216 | tf_op jit(solution)/shard_map/psum | solution.py:188
  122.2 11.1 %copy-start.2 = (bf16[1024,96]{1,0:T(8,128)(2,1)S(1)}, bf16[1024,96]{1,0:T(8,128)(2,1)}, u32[]{:S(2)}) copy-start(bf16[1024,96]{1,0:T(8,128)(2,1)} %copy-done.1) | copy-start | bytes 589828
  122.2 11.1 %copy-start.4 = (bf16[1024,96]{1,0:T(8,128)(2,1)S(1)}, bf16[1024,96]{1,0:T(8,128)(2,1)}, u32[]{:S(2)}) copy-start(bf16[1024,96]{1,0:T(8,128)(2,1)} %copy-done.3) | copy-start | bytes 589828
  122.2 11.1 %copy-start.6 = (bf16[2,512,96]{2,1,0:T(8,128)(2,1)S(1)}, bf16[2,512,96]{2,1,0:T(8,128)(2,1)}, u32[]{:S(2)}) copy-start(bf16[2,512,96]{2,1,0:T(8,128)(2,1)} %copy-done.5) | copy-start | bytes 589828
  146.2 65.3 %copy-start.9 = (f32[128,1536]{1,0:T(8,128)S(1)}, f32[128,1536]{1,0:T(8,128)}, u32[]{:S(2)}) copy-start(f32[128,1536]{1,0:T(8,128)} %get-tuple-element.300) | copy-start | bytes 2359300
  146.3 65.3 %copy-start.10 = (bf16[128,1536]{1,0:T(8,128)(2,1)S(1)}, bf16[128,1536]{1,0:T(8,128)(2,1)}, u32[]{:S(2)}) copy-start(bf16[128,1536]{1,0:T(8,128)(2,1)} %get-tuple-element.318) | copy-start | bytes 1179652
  146.3 65.3 %copy-start.52 = (pred[128]{0:T(512)(128)(4,1)S(1)}, pred[128]{0:T(512)(128)(4,1)}, u32[]{:S(2)}) copy-start(pred[128]{0:T(512)(128)(4,1)} %add_compare_fusion) | copy-start | bytes 388
  150.8 61.8 %copy-start.49 = (f32[1536]{0:T(1024)S(1)}, f32[1536]{0:T(1024)}, u32[]{:S(2)}) copy-start(f32[1536]{0:T(1024)} %get-tuple-element.235) | copy-start | bytes 18436
  156.6 118.6 %all-to-all-start.4 = ((bf16[8,2,6144]{2,1,0:T(2,128)(2,1)}), bf16[8,2,6144]{2,1,0:T(2,128)(2,1)}, u32[]{:S(2)}, u32[]{:S(2)}) async-start(bf16[8,2,6144]{2,1,0:T(2,128)(2,1)} %reshape.178), calls=%async_computation.4 | async-start | bytes 393216 | tf_op jit(solution)/shard_map/all_to_all | solution.py:181
  161.1 148.4 %all-reduce.3.cloned.1.call-start = ((), (), s32[]{:S(2)}) async-start(), calls=%async_computation.7 | async-start | bytes 589824 | tf_op jit(solution)/shard_map/psum | solution.py:187
  (42 other events, 296.1 us)
Sparse Core Ops, SparseCore 0:
  107.1 102.5 reduce-scatter.1
Sparse Core Ops, SparseCore 1:
  129.3 144.3 all-reduce.4
  276.5 32.9 all-reduce.2
